TPU v7x, 32 devices: a whole 2x2x4 slice. The times are simulated.
32 devices in a mesh: expert: 8 (over z, y), mp: 4 (over x, core).
Axes of the slice: x: 2, y: 2, z: 4, core: 2. Of those that a mesh axis runs over, the one named last changes fastest.
Arguments:
- queries: bfloat16 [256, 48, 128], P('expert', 'mp'), may hold values from -140 to 140
- k_cache: bfloat16 [256, 8, 128, 128], P('expert', 'mp'), may hold values from -5 to 5
- v_cache: bfloat16 [256, 8, 128, 128], P('expert', 'mp'), may hold values from -6 to 6
- lengths: int32 [256], P('expert'), may hold values from 2 to 128
- moe_input: bfloat16 [256, 6144], P('expert', 'mp'), may hold values from -40 to 40
- norm_gain: float32 [6144], P('mp'), may hold values from 0.5 to 1.5
- expert_ids: int32 [256, 2], P('expert'), may hold values from 0 to 7, all different within a row; in each aligned block of 32 rows (0 to 31, 32 to 63, ...) at most 16 rows name the same one
- combine_weights: float32 [256, 2], P('expert'), may hold values from 0.1 to 1
- capacity: int32 [8], replicated, may hold values from 8 to 16
- w_gate: bfloat16 [8, 6144, 8192], P('expert', None, 'mp'), may hold values from -0.078125 to 0.078125
- w_up: bfloat16 [8, 6144, 8192], P('expert', None, 'mp'), may hold values from -0.078125 to 0.078125
- w_down: bfloat16 [8, 8192, 6144], P('expert', 'mp'), may hold values from -0.0625 to 0.0625
Outputs:
- context: bfloat16 [256, 48, 128], P('expert', 'mp')
- layer_out: bfloat16 [256, 6144], P('expert', 'mp')
Inputs may be any that keep to these rules, and one draw needn't show every extreme that they name: `expert_ids`: within each aligned block of 32 tokens, no expert is named by more than 16 tokens; the 2 ids of a token differ.
All inputs are finite; a program needn't handle non-finite values.
Results may differ from a plain program's by a relative error of at most 0.007.
Values may be sent and summed in bfloat16 or wider, within the bound.
No kernel may reach another device: no remote copies, remote signals or barrier semaphores. Data moves between devices by JAX's collectives and lax.ppermute only.
A program may use at most 128 MiB of HBM per device.

v0:
```python
import jax
import jax.numpy as jnp
from jax import lax
from jax.sharding import PartitionSpec as P

D = 6144
EXPERTS = 8
TOP = 2


def on_device(
    queries,
    k_cache,
    v_cache,
    lengths,
    moe_input,
    norm_gain,
    expert_ids,
    combine_weights,
    capacity,
    w_gate,
    w_up,
    w_down,
):
    seq_count, head_count, head_size = queries.shape
    kv_count = k_cache.shape[1]
    group_size = head_count // kv_count
    queries_grouped = queries.reshape(seq_count, kv_count, group_size, head_size)
    scores = jnp.einsum(
        "bjgd,bjpd->bjgp", queries_grouped, k_cache, preferred_element_type=jnp.float32
    ) * head_size ** (-0.5)
    positions = jnp.arange(k_cache.shape[2])
    live_mask = positions[None, :] < lengths[:, None]
    scores = jnp.where(live_mask[:, None, None, :], scores, -jnp.inf)
    top_score = jnp.max(scores, axis=-1, keepdims=True)
    expo = jnp.exp(scores - top_score)
    probs = (expo / jnp.sum(expo, axis=-1, keepdims=True)).astype(jnp.bfloat16)
    context = jnp.einsum("bjgp,bjpd->bjgd", probs, v_cache, preferred_element_type=jnp.float32)
    context = context.astype(jnp.bfloat16).reshape(seq_count, head_count, head_size)
    tok_rows, feat_width = moe_input.shape
    experts_total = lax.axis_size("expert")
    split_count = experts_total // EXPERTS
    slot_count = tok_rows // 2
    residual = moe_input.astype(jnp.float32)
    square_sum = lax.psum(jnp.sum(residual * residual, axis=1), "mp")
    normed = (residual * lax.rsqrt(square_sum / D + 1e-05)[:, None] * norm_gain[None, :]).astype(
        jnp.bfloat16
    )
    flat_ids = expert_ids.reshape(-1)
    one_hot = (flat_ids[:, None] == jnp.arange(EXPERTS)[None, :]).astype(jnp.int32)
    earlier = jnp.cumsum(one_hot, axis=0) - one_hot
    slot_rank = jnp.sum(earlier * one_hot, axis=1)
    limits = jnp.sum(one_hot * capacity[None, :], axis=1)
    kept_mask = slot_rank < limits
    slot_id = flat_ids * slot_count + slot_rank
    select = (jnp.arange(EXPERTS * slot_count)[:, None] == slot_id[None, :]) & kept_mask[None, :]
    chosen = select.reshape(EXPERTS * slot_count, tok_rows, TOP).sum(axis=-1).astype(jnp.bfloat16)
    packed = jnp.dot(chosen, normed, preferred_element_type=jnp.float32).astype(jnp.bfloat16)
    packed_view = packed.reshape(EXPERTS, 1, slot_count, feat_width)
    outgoing = jnp.broadcast_to(
        packed_view, (EXPERTS, split_count, slot_count, feat_width)
    ).reshape(experts_total, slot_count, feat_width)
    arrived = lax.all_to_all(outgoing, "expert", split_axis=0, concat_axis=0, tiled=True)
    slot_rows = arrived.reshape(experts_total * slot_count, feat_width)
    gate_matrix = w_gate[0]
    up_matrix = w_up[0]
    piece = lax.all_gather(slot_rows, "mp", axis=1, tiled=True)
    gate_sum = jnp.dot(piece, gate_matrix, preferred_element_type=jnp.float32)
    up_sum = jnp.dot(piece, up_matrix, preferred_element_type=jnp.float32)
    hidden = (jax.nn.silu(gate_sum) * up_sum).astype(jnp.bfloat16)
    down_terms = jnp.dot(hidden, w_down[0], preferred_element_type=jnp.float32)
    result = lax.psum_scatter(
        down_terms.astype(jnp.bfloat16), "mp", scatter_dimension=1, tiled=True
    ).astype(jnp.float32)
    result = result.reshape(experts_total, slot_count, feat_width)
    returned = lax.all_to_all(
        result.astype(jnp.bfloat16), "expert", split_axis=0, concat_axis=0, tiled=True
    ).astype(result.dtype)
    gathered = returned.reshape(EXPERTS, split_count, slot_count, feat_width).sum(axis=1)
    weighted = select.astype(jnp.float32) * combine_weights.reshape(-1)[None, :]
    weighted = weighted.reshape(EXPERTS * slot_count, tok_rows, TOP).sum(axis=-1)
    added = jnp.dot(
        weighted.T,
        gathered.reshape(EXPERTS * slot_count, feat_width),
        precision=lax.Precision.HIGHEST,
        preferred_element_type=jnp.float32,
    )
    layer_out = (residual + added).astype(jnp.bfloat16)
    return (context, layer_out)


def solution(mesh):
    in_specs = (
        P("expert", "mp", None),
        P("expert", "mp", None, None),
        P("expert", "mp", None, None),
        P("expert"),
        P("expert", "mp"),
        P("mp"),
        P("expert", None),
        P("expert", None),
        P(),
        P("expert", None, "mp"),
        P("expert", None, "mp"),
        P("expert", "mp", None),
    )
    out_specs = (P("expert", "mp", None), P("expert", "mp"))
    return jax.shard_map(
        on_device, mesh=mesh, in_specs=in_specs, out_specs=out_specs, check_vma=False
    )
```

profile of v0, /device:TPU:0, one launch (start us, length us, event | category | flops | bytes accessed | tf_op | source)
XLA Modules:
  0.0 139.0 jit_solution(575278981776266259)
XLA Ops:
  7.2 0.9 copy.35
  8.1 0.1 eq.31
  8.3 0.1 reduce_window_sum.11
  8.4 0.8 select_reduce_fusion.1
  9.2 0.1 reduce_sum.64
  9.4 0.1 reduce_sum.66
  9.6 0.1 copy.37
  9.7 0.7 multiply_add_fusion
  10.3 1.0 fusion.28
  11.4 8.4 %psum.7 = f32[32]{0:T(128)S(1)} all-reduce(f32[32]{0:T(128)S(1)} %fusion.28), channel_id=1, replica_groups=mesh['expert'=8,'mp'=4] {'mp'}, use_global_device_ids=true, to_apply=%region_8.9 | all-reduce | flops 32 | bytes 256 | tf_op jit(solution)/shard_map/psum | solution.py:45
  19.8 1.2 convolution_convert_fusion
  21.0 16.6 %all_to_all.10 = bf16[8,16,1536]{2,1,0:T(8,128)(2,1)} all-to-all(bf16[8,16,1536]{2,1,0:T(8,128)(2,1)S(1)} %bitcast.33), channel_id=1, replica_groups=mesh['expert'=8,'mp'=4] {'expert'}, dimensions={0} | all-to-all | bytes 786432 | tf_op jit(solution)/shard_map/all_to_all | solution.py:63
  37.7 18.4 %all-gather.2.cloned.1.call-done = bf16[128,6144]{1,0:T(8,128)(2,1)} async-done(((bf16[128,1536]{1,0:T(8,128)(2,1)}), bf16[128,6144]{1,0:T(8,128)(2,1)}) %all-gather.2.cloned.1.call-update) | async-done | bytes 1572880 | tf_op jit(solution)/shard_map/all_gather | solution.py:67
  56.1 10.4 %fusion.5 = f32[128,2048]{1,0:T(8,128)S(1)} fusion(bf16[128,6144]{1,0:T(8,128)(2,1)} %all-gather.2.cloned.1.call-done, bf16[1,6144,2048]{2,1,0:T(8,128)(2,1)} %param.21), kind=kOutput, calls=%fused_computation.5 | convolution fusion | flops 3221225472 | bytes 27787264 | tf_op jit(solution)/shard_map/dot_general | solution.py:68
  66.6 19.4 %fusion.7 = bf16[128,6144]{1,0:T(8,128)(2,1)} fusion(bf16[1,2048,6144]{2,1,0:T(8,128)(2,1)} %param.23, bf16[128,6144]{1,0:T(8,128)(2,1)} %all-gather.2.cloned.1.call-done, bf16[1,6144,2048]{2,1,0:T(8,128)(2,1)} %param.22, f32[128,2048]{1,0:T(8,128)S(1)} %fusion.5), kind=kOutput, calls=%fused_computation.7 | convolution fusion | flops 6444810240 | bytes 54525952 | tf_op jit(solution)/shard_map/dot_general | solution.py:71
  86.1 28.1 %reduce-scatter.2.cloned.1.call-done = bf16[128,1536]{1,0:T(8,128)(2,1)} async-done(((bf16[128,6144]{1,0:T(8,128)(2,1)}), bf16[128,1536]{1,0:T(8,128)(2,1)}) %reduce-scatter.2.cloned.1.call-update) | async-done | bytes 393232 | tf_op jit(solution)/shard_map/reduce_scatter | solution.py:72
  114.2 5.5 %all-to-all-start.1 = ((bf16[8,16,1536]{2,1,0:T(8,128)(2,1)}), bf16[8,16,1536]{2,1,0:T(8,128)(2,1)S(1)}, u32[]{:S(2)}, u32[]{:S(2)}) async-start(bf16[8,16,1536]{2,1,0:T(8,128)(2,1)} %bitcast.34), calls=%async_computation.2 | async-start | bytes 786432 | tf_op jit(solution)/shard_map/all_to_all | solution.py:76
  119.7 1.2 fusion.20
  120.9 0.3 fusion.40
  121.2 2.5 %convolution_convert_fusion.1 = bf16[32,2,6,128]{3,2,1,0:T(8,128)(2,1)S(1)} fusion(bf16[32,2,128,128]{3,2,1,0:T(8,128)(2,1)} %param.14, f32[32,2,6]{2,1,0:T(2,128)S(1)} %fusion.40, f32[32,2,6,128]{3,2,1,0:T(8,128)S(1)} %fusion.20), kind=kOutput, calls=%fused_computation.17 | convolution fusion | flops 12780031 | bytes 2393600 | tf_op jit(solution)/shard_map/bjgp,bjpd->bjgd/dot_general | solution.py:38
  123.7 0.7 copy.34
  124.3 0.1 select_reduce_fusion
  124.4 6.8 %all-to-all-done.1 = bf16[8,16,1536]{2,1,0:T(8,128)(2,1)S(1)} async-done(((bf16[8,16,1536]{2,1,0:T(8,128)(2,1)}), bf16[8,16,1536]{2,1,0:T(8,128)(2,1)S(1)}, u32[]{:S(2)}, u32[]{:S(2)}) %all-to-all-start.1) | async-done | bytes 393248 | tf_op jit(solution)/shard_map/all_to_all | solution.py:76
  131.2 0.9 fusion.18
  (20 shorter events, 0.5 us)
Async XLA Ops:
  7.2 112.5 %copy-start = (bf16[32,2,128,128]{3,2,1,0:T(8,128)(2,1)S(1)}, bf16[32,2,128,128]{3,2,1,0:T(8,128)(2,1)}, u32[]{:S(2)}) copy-start(bf16[32,2,128,128]{3,2,1,0:T(8,128)(2,1)} %param.13) | copy-start | bytes 6291460
  7.2 49.0 %all-gather.2.cloned.1.call-start = ((), (), s32[]{:S(2)}) async-start(), calls=%async_computation.3 | async-start | bytes 1966080 | tf_op jit(solution)/shard_map/all_gather | solution.py:67
  37.7 76.5 %reduce-scatter.2.cloned.1.call-start = ((), (), s32[]{:S(2)}) async-start(), calls=%async_computation.4 | async-start | bytes 1966080 | tf_op jit(solution)/shard_map/reduce_scatter | solution.py:72
  66.6 19.4 %copy-start.4 = (s32[32]{0:T(128)S(1)}, s32[32]{0:T(128)}, u32[]{:S(2)}) copy-start(s32[32]{0:T(128)} %param.15) | copy-start | bytes 388
  86.0 33.7 %copy-start.2 = (bf16[32,12,128]{2,0,1:T(8,128)(2,1)S(1)}, bf16[32,12,128]{2,0,1:T(8,128)(2,1)}, u32[]{:S(2)}) copy-start(bf16[32,12,128]{2,0,1:T(8,128)(2,1)} %param.12) | copy-start | bytes 294916
  114.2 17.1 %all-to-all-start.1 = ((bf16[8,16,1536]{2,1,0:T(8,128)(2,1)}), bf16[8,16,1536]{2,1,0:T(8,128)(2,1)S(1)}, u32[]{:S(2)}, u32[]{:S(2)}) async-start(bf16[8,16,1536]{2,1,0:T(8,128)(2,1)} %bitcast.34), calls=%async_computation.2 | async-start | bytes 786432 | tf_op jit(solution)/shard_map/all_to_all | solution.py:76
  120.9 3.5 %copy-start.3 = (f32[32,2]{0,1:T(2,128)S(1)}, f32[32,2]{0,1:T(2,128)}, u32[]{:S(2)}) copy-start(f32[32,2]{0,1:T(2,128)} %param.19) | copy-start | bytes 772
  120.9 10.4 %copy-start.1 = (bf16[32,1536]{1,0:T(8,128)(2,1)S(1)}, bf16[32,1536]{1,0:T(8,128)(2,1)}, u32[]{:S(2)}) copy-start(bf16[32,1536]{1,0:T(8,128)(2,1)} %param.16) | copy-start | bytes 294916
Sparse Core Ops, SparseCore 0:
  37.8 18.3 all-gather.1
  86.1 27.9 reduce-scatter.1
where the time goes:
time: 139 us
  waiting for transfers between devices  53.3 us (38%)
  matrix products  35.6 us (26%)
  blocking collectives  25 us (18%)
  between operations  14.1 us (10%)
  starting transfers between devices  5.59 us (4%)
  other arithmetic  3.26 us (2%)
  local copies, waits for them, and re-layouts  2.08 us (1%)
    reduce_scatter x1, waiting for transfers between devices, on_device(): lax.psum_scatter(down_terms.astype(jnp.bfloat16), 'mp', scatter_dimension...  28.1 us
    dot_general x1, matrix products, on_device(): down_terms = jnp.dot(hidden, w_down[0], preferred_element_type=jnp.float32)  19.4 us
    all_gather x1, waiting for transfers between devices, on_device(): piece = lax.all_gather(slot_rows, 'mp', axis=1, tiled=True)  18.4 us
    all_to_all x1, blocking collectives, on_device(): lax.all_to_all(outgoing, 'expert', split_axis=0, concat_axis=0, tiled=True)  16.6 us
    dot_general x1, matrix products, on_device(): gate_sum = jnp.dot(piece, gate_matrix, preferred_element_type=jnp.float32)  10.4 us
    psum x1, blocking collectives, on_device(): square_sum = lax.psum(jnp.sum(residual * residual, axis=1), 'mp')  8.37 us
    all_to_all x1, waiting for transfers between devices, on_device(): lax.all_to_all(result.astype(jnp.bfloat16), 'expert', split_axis=0, conca...  6.79 us
    all_to_all x1, starting transfers between devices, on_device(): lax.all_to_all(result.astype(jnp.bfloat16), 'expert', split_axis=0, conca...  5.51 us
  transfers between devices with their start and end apart: 3, of which 3 were waited for; matrix products, arithmetic and copies ran while one was open for 3% of the time, Pallas kernels for 0%

commit v1 on v0

--- a/solution.py
+++ b/solution.py
@@ -42,7 +42,7 @@
     split_count = experts_total // EXPERTS
     slot_count = tok_rows // 2
     residual = moe_input.astype(jnp.float32)
-    square_sum = lax.psum(jnp.sum(residual * residual, axis=1), "mp")
+    square_sum = jnp.sum(lax.all_gather(jnp.sum(residual * residual, axis=1), "mp"), axis=0)
     normed = (residual * lax.rsqrt(square_sum / D + 1e-05)[:, None] * norm_gain[None, :]).astype(
         jnp.bfloat16
     )

time: 139 us -> 142 us (1.022)
  local copies, waits for them, and re-layouts: 2.08 us -> 3.65 us
    psum x1 -> x0, blocking collectives: 8.37 us -> none  [on_device(): square_sum = lax.psum(jnp.sum(residual * residual, axis=1), 'mp')]
    unnamed x0 -> x1, blocking collectives: none -> 8.34 us
    unnamed x11 -> x14, local copies, waits for them, and re-layouts: 0.93 us -> 2.41 us
where the time goes in v1:
time: 142 us; the launch traced here: 141 us
  waiting for transfers between devices  53.4 us (38%)
  matrix products  35.6 us (25%)
  blocking collectives  24.9 us (18%)
  between operations  14.8 us (10%)
  starting transfers between devices  5.6 us (4%)
  local copies, waits for them, and re-layouts  3.65 us (3%)
  other arithmetic  3.28 us (2%)
    reduce_scatter x1, waiting for transfers between devices, on_device(): lax.psum_scatter(down_terms.astype(jnp.bfloat16), 'mp', scatter_dimension...  28.1 us
    dot_general x1, matrix products, on_device(): down_terms = jnp.dot(hidden, w_down[0], preferred_element_type=jnp.float32)  19.4 us
    all_gather x1, waiting for transfers between devices, on_device(): piece = lax.all_gather(slot_rows, 'mp', axis=1, tiled=True)  18.5 us
    all_to_all x1, blocking collectives, on_device(): lax.all_to_all(outgoing, 'expert', split_axis=0, concat_axis=0, tiled=True)  16.6 us
    dot_general x1, matrix products, on_device(): gate_sum = jnp.dot(piece, gate_matrix, preferred_element_type=jnp.float32)  10.4 us
    unnamed x1, blocking collectives  8.34 us
    all_to_all x1, waiting for transfers between devices, on_device(): lax.all_to_all(result.astype(jnp.bfloat16), 'expert', split_axis=0, conca...  6.8 us
    all_to_all x1, starting transfers between devices, on_device(): lax.all_to_all(result.astype(jnp.bfloat16), 'expert', split_axis=0, conca...  5.52 us
  transfers between devices with their start and end apart: 3, of which 3 were waited for; matrix products, arithmetic and copies ran while one was open for 3% of the time, Pallas kernels for 0%

profile of v1, /device:TPU:0, one launch (start us, length us, event | category | flops | bytes accessed | tf_op | source)
XLA Modules:
  0.0 141.3 jit_solution(1134338209041496504)
XLA Ops:
  7.2 0.9 copy.35
  8.1 0.1 eq.31
  8.3 0.1 reduce_window_sum.11
  8.4 0.8 select_reduce_fusion.1
  9.3 0.1 reduce_sum.73
  9.4 0.1 reduce_sum.75
  9.7 0.7 multiply_add_fusion
  10.4 1.0 fusion.28
  11.4 1.2 dynamic-slice
  13.3 0.2 dynamic-update-slice
  13.5 8.3 %all-reduce = f32[128]{0:T(128)S(1)} all-reduce(f32[128]{0:T(128)S(1)} %dynamic-update-slice), channel_id=2, replica_groups=mesh['expert'=8,'mp'=4] {'mp'}, use_global_device_ids=true, to_apply=%add | all-reduce | flops 128 | bytes 1024
  22.1 1.2 convolution_convert_fusion
  23.3 16.6 %all_to_all.10 = bf16[8,16,1536]{2,1,0:T(8,128)(2,1)} all-to-all(bf16[8,16,1536]{2,1,0:T(8,128)(2,1)S(1)} %bitcast.34), channel_id=1, replica_groups=mesh['expert'=8,'mp'=4] {'expert'}, dimensions={0} | all-to-all | bytes 786432 | tf_op jit(solution)/shard_map/all_to_all | solution.py:63
  39.9 18.5 %all-gather.3.cloned.1.call-done = bf16[128,6144]{1,0:T(8,128)(2,1)} async-done(((bf16[128,1536]{1,0:T(8,128)(2,1)}), bf16[128,6144]{1,0:T(8,128)(2,1)}) %all-gather.3.cloned.1.call-update) | async-done | bytes 1572880 | tf_op jit(solution)/shard_map/all_gather | solution.py:67
  58.4 10.4 %fusion.5 = f32[128,2048]{1,0:T(8,128)S(1)} fusion(bf16[128,6144]{1,0:T(8,128)(2,1)} %all-gather.3.cloned.1.call-done, bf16[1,6144,2048]{2,1,0:T(8,128)(2,1)} %param.21), kind=kOutput, calls=%fused_computation.5 | convolution fusion | flops 3221225472 | bytes 27787264 | tf_op jit(solution)/shard_map/dot_general | solution.py:68
  68.8 19.4 %fusion.7 = bf16[128,6144]{1,0:T(8,128)(2,1)} fusion(bf16[1,2048,6144]{2,1,0:T(8,128)(2,1)} %param.23, bf16[128,6144]{1,0:T(8,128)(2,1)} %all-gather.3.cloned.1.call-done, bf16[1,6144,2048]{2,1,0:T(8,128)(2,1)} %param.22, f32[128,2048]{1,0:T(8,128)S(1)} %fusion.5), kind=kOutput, calls=%fused_computation.7 | convolution fusion | flops 6444810240 | bytes 54525952 | tf_op jit(solution)/shard_map/dot_general | solution.py:71
  88.3 28.1 %reduce-scatter.2.cloned.1.call-done = bf16[128,1536]{1,0:T(8,128)(2,1)} async-done(((bf16[128,6144]{1,0:T(8,128)(2,1)}), bf16[128,1536]{1,0:T(8,128)(2,1)}) %reduce-scatter.2.cloned.1.call-update) | async-done | bytes 393232 | tf_op jit(solution)/shard_map/reduce_scatter | solution.py:72
  116.4 5.5 %all-to-all-start.1 = ((bf16[8,16,1536]{2,1,0:T(8,128)(2,1)}), bf16[8,16,1536]{2,1,0:T(8,128)(2,1)S(1)}, u32[]{:S(2)}, u32[]{:S(2)}) async-start(bf16[8,16,1536]{2,1,0:T(8,128)(2,1)} %bitcast.35), calls=%async_computation.2 | async-start | bytes 786432 | tf_op jit(solution)/shard_map/all_to_all | solution.py:76
  122.0 1.2 fusion.20
  123.2 0.3 fusion.40
  123.4 2.5 %convolution_convert_fusion.1 = bf16[32,2,6,128]{3,2,1,0:T(8,128)(2,1)S(1)} fusion(bf16[32,2,128,128]{3,2,1,0:T(8,128)(2,1)} %param.14, f32[32,2,6]{2,1,0:T(2,128)S(1)} %fusion.40, f32[32,2,6,128]{3,2,1,0:T(8,128)S(1)} %fusion.20), kind=kOutput, calls=%fused_computation.17 | convolution fusion | flops 12780031 | bytes 2393600 | tf_op jit(solution)/shard_map/bjgp,bjpd->bjgd/dot_general | solution.py:38
  126.0 0.7 copy.34
  126.7 6.8 %all-to-all-done.1 = bf16[8,16,1536]{2,1,0:T(8,128)(2,1)S(1)} async-done(((bf16[8,16,1536]{2,1,0:T(8,128)(2,1)}), bf16[8,16,1536]{2,1,0:T(8,128)(2,1)S(1)}, u32[]{:S(2)}, u32[]{:S(2)}) %all-to-all-start.1) | async-done | bytes 393248 | tf_op jit(solution)/shard_map/all_to_all | solution.py:76
  133.5 0.9 fusion.18
  (25 shorter events, 0.8 us)
Async XLA Ops:
  7.2 114.8 %copy-start = (bf16[32,2,128,128]{3,2,1,0:T(8,128)(2,1)S(1)}, bf16[32,2,128,128]{3,2,1,0:T(8,128)(2,1)}, u32[]{:S(2)}) copy-start(bf16[32,2,128,128]{3,2,1,0:T(8,128)(2,1)} %param.13) | copy-start | bytes 6291460
  7.2 51.2 %all-gather.3.cloned.1.call-start = ((), (), s32[]{:S(2)}) async-start(), calls=%async_computation.3 | async-start | bytes 1966080 | tf_op jit(solution)/shard_map/all_gather | solution.py:67
  39.9 76.6 %reduce-scatter.2.cloned.1.call-start = ((), (), s32[]{:S(2)}) async-start(), calls=%async_computation.4 | async-start | bytes 1966080 | tf_op jit(solution)/shard_map/reduce_scatter | solution.py:72
  68.8 19.4 %copy-start.4 = (s32[32]{0:T(128)S(1)}, s32[32]{0:T(128)}, u32[]{:S(2)}) copy-start(s32[32]{0:T(128)} %param.15) | copy-start | bytes 388
  88.2 33.8 %copy-start.2 = (bf16[32,12,128]{2,0,1:T(8,128)(2,1)S(1)}, bf16[32,12,128]{2,0,1:T(8,128)(2,1)}, u32[]{:S(2)}) copy-start(bf16[32,12,128]{2,0,1:T(8,128)(2,1)} %param.12) | copy-start | bytes 294916
  116.4 17.1 %all-to-all-start.1 = ((bf16[8,16,1536]{2,1,0:T(8,128)(2,1)}), bf16[8,16,1536]{2,1,0:T(8,128)(2,1)S(1)}, u32[]{:S(2)}, u32[]{:S(2)}) async-start(bf16[8,16,1536]{2,1,0:T(8,128)(2,1)} %bitcast.35), calls=%async_computation.2 | async-start | bytes 786432 | tf_op jit(solution)/shard_map/all_to_all | solution.py:76
  123.2 3.5 %copy-start.3 = (f32[32,2]{0,1:T(2,128)S(1)}, f32[32,2]{0,1:T(2,128)}, u32[]{:S(2)}) copy-start(f32[32,2]{0,1:T(2,128)} %param.19) | copy-start | bytes 772
  123.2 10.4 %copy-start.1 = (bf16[32,1536]{1,0:T(8,128)(2,1)S(1)}, bf16[32,1536]{1,0:T(8,128)(2,1)}, u32[]{:S(2)}) copy-start(bf16[32,1536]{1,0:T(8,128)(2,1)} %param.16) | copy-start | bytes 294916
Sparse Core Ops, SparseCore 0:
  40.0 18.3 all-gather.2
  88.4 28.0 reduce-scatter.1
